TPU v7x, 128 devices: a whole 4x4x4 slice. The times are simulated.
128 devices in a mesh: dp: 16 (over z_hi, x, core), tensor: 8 (over z_lo, y).
Axes of the slice: x: 4, y: 4, z: 4 (z_hi: 2, z_lo: 2; z = z_hi * 2 + z_lo), core: 2. Of those that a mesh axis runs over, the one named last changes fastest.
Arguments:
- tokens: bfloat16 [16384, 8192], P('dp', 'tensor'), may hold values from -6 to 6
- ref_gain: float32 [8192], P('tensor'), may hold values from 0.1 to 1.9
- ref_weight: bfloat16 [8192, 512], P('tensor'), may hold values from -0.0625 to 0.0625
- pol_gain: float32 [8192], replicated, may hold values from 0.1 to 1.9
- pol_weight: bfloat16 [8192, 512], P('dp'), may hold values from -0.0625 to 0.0625
- lengths: int32 [16, 8, 16], P('dp', 'tensor'), may hold values from 1 to 16, 128 in all within a row
- bins: int32 [16, 8, 16], P('dp', 'tensor'), may hold values from 0 to 15, each once within a row
- advantage: float32 [16, 8, 16], P('dp', 'tensor'), may hold values from -4 to 4
- logprob_gap: float32 [16384], P(('dp', 'tensor')), may hold values from -1 to 1
- cotangent: bfloat16 [16, 8, 256, 512], P('dp', 'tensor'), may hold values from -6 to 6
Outputs:
- policy_values: bfloat16 [16, 8, 256, 512], P('dp', 'tensor')
- grad_weight: float32 [8192, 512], P(('dp', 'tensor'))
Inputs may be any that keep to these rules, and one draw needn't show every extreme that they name: `lengths`: lengths of the 16 sequences of one run, in the order in which they lie in it; they sum to 128, and the longest of every run is exactly 16. The sequences of one run go to distinct bins: each bin takes exactly one sequence of every run.
All inputs are finite; a program needn't handle non-finite values.
Results may differ from a plain program's by a relative error of at most 0.015.
Values may be sent and summed in bfloat16 or wider, within the bound.
A program may use at most 64 MiB of HBM per device.

v0:
```python
import math

import jax
import jax.numpy as jnp
from jax import lax
from jax.sharding import PartitionSpec as P

EPS = 1e-06
BETA = 1.0


def rounded(values):
    return lax.optimization_barrier(values.astype(jnp.bfloat16)).astype(jnp.float32)


def on_device(
    tokens,
    ref_gain,
    ref_weight,
    pol_gain,
    pol_weight,
    lengths,
    bins,
    advantage,
    logprob_gap,
    cotangent,
):
    tensor_count = lax.axis_size("tensor")
    dp_count = lax.axis_size("dp")
    group_rows = tokens.shape[0]
    own_rows = group_rows // tensor_count
    slot_count = cotangent.shape[2]
    span_rows = slot_count // dp_count
    model_width = pol_gain.shape[0]
    value_width = ref_weight.shape[1]
    scaled = (tokens.astype(jnp.float32) * ref_gain[None, :]).astype(jnp.bfloat16)
    partial_value = rounded(jnp.dot(scaled, ref_weight, preferred_element_type=jnp.float32))
    summed = lax.psum(partial_value.astype(jnp.bfloat16), "tensor").astype(jnp.float32)
    owned_sum = lax.dynamic_slice_in_dim(summed, lax.axis_index("tensor") * own_rows, own_rows, 0)
    full_rows = lax.all_to_all(tokens, "tensor", split_axis=0, concat_axis=1, tiled=True)
    row_power = jnp.mean(jnp.square(full_rows.astype(jnp.float32)), axis=1)
    ref_values = (owned_sum * lax.rsqrt(row_power + EPS)[:, None]).astype(jnp.bfloat16)
    seq_lens = lengths.reshape(-1)
    seq_bins = bins.reshape(-1)
    seq_adv = advantage.reshape(-1)
    seq_starts = jnp.cumsum(seq_lens) - seq_lens
    chosen = seq_bins[None, :] == jnp.arange(dp_count, dtype=jnp.int32)[:, None]
    bin_len = jnp.sum(jnp.where(chosen, seq_lens[None, :], 0), axis=1)
    bin_start = jnp.sum(jnp.where(chosen, seq_starts[None, :], 0), axis=1)
    bin_adv = jnp.sum(jnp.where(chosen, seq_adv[None, :], jnp.float32(0.0)), axis=1)
    offsets = jnp.arange(span_rows, dtype=jnp.int32)
    usable = offsets[None, :] < bin_len[:, None]
    row_picks = jnp.clip(bin_start[:, None] + offsets[None, :], 0, own_rows - 1)
    send_rows = jnp.where(usable[:, :, None], full_rows[row_picks], jnp.zeros((), jnp.bfloat16))
    send_ref = jnp.where(usable[:, :, None], ref_values[row_picks], jnp.zeros((), jnp.bfloat16))
    len_float = bin_len.astype(jnp.float32)[:, None]
    importance = jnp.minimum(jnp.exp(logprob_gap[row_picks]), jnp.float32(2.0))
    coef_adv = jnp.where(
        usable, bin_adv[:, None] * importance / len_float, jnp.float32(0.0)
    ).astype(jnp.bfloat16)
    coef_pull = jnp.where(usable, BETA / len_float, jnp.float32(0.0)).astype(jnp.bfloat16)
    got_rows, got_ref, got_adv, got_pull = (
        lax.all_to_all(send_rows, "dp", split_axis=0, concat_axis=0, tiled=True),
        lax.all_to_all(send_ref, "dp", split_axis=0, concat_axis=0, tiled=True),
        lax.all_to_all(coef_adv, "dp", split_axis=0, concat_axis=0, tiled=True),
        lax.all_to_all(coef_pull, "dp", split_axis=0, concat_axis=0, tiled=True),
    )
    packed_rows = got_rows.reshape(slot_count, model_width)
    power = jnp.mean(jnp.square(packed_rows.astype(jnp.float32)), axis=1)
    normed = (
        packed_rows.astype(jnp.float32) * lax.rsqrt(power + EPS)[:, None] * pol_gain[None, :]
    ).astype(jnp.bfloat16)
    packed_ref = got_ref.reshape(slot_count, value_width).astype(jnp.float32)
    adv_column = got_adv.reshape(slot_count, 1).astype(jnp.float32)
    pull_column = got_pull.reshape(slot_count, 1).astype(jnp.float32)
    upstream = cotangent.reshape(slot_count, value_width).astype(jnp.float32)
    factor = 1.0 / math.sqrt(dp_count * tensor_count * seq_lens.shape[0])
    feature_block = normed
    values = jnp.dot(
        feature_block,
        lax.all_gather(pol_weight, "dp", axis=0, tiled=True),
        preferred_element_type=jnp.float32,
    )
    slope = (adv_column * upstream + pull_column * (values - packed_ref)).astype(jnp.bfloat16)
    feature_block = normed
    grad_weight = lax.psum_scatter(
        lax.dot_general(
            feature_block, slope, (((0,), (0,)), ((), ())), preferred_element_type=jnp.float32
        )
        * factor,
        ("dp", "tensor"),
        scatter_dimension=0,
        tiled=True,
    )
    policy_values = values.astype(jnp.bfloat16).reshape(1, 1, slot_count, value_width)
    return (policy_values, grad_weight)


def solution(mesh):
    in_specs = (
        P("dp", "tensor"),
        P("tensor"),
        P("tensor", None),
        P(),
        P("dp", None),
        P("dp", "tensor", None),
        P("dp", "tensor", None),
        P("dp", "tensor", None),
        P(("dp", "tensor")),
        P("dp", "tensor", None, None),
    )
    out_specs = (P("dp", "tensor", None, None), P(("dp", "tensor"), None))
    return jax.shard_map(
        on_device, mesh=mesh, in_specs=in_specs, out_specs=out_specs, check_vma=False
    )
```

profile of v0, /device:TPU:24, one launch (start us, length us, event | category | flops | bytes accessed | tf_op | source)
XLA Modules:
  0.0 847.1 jit_solution(14189858339868962872)
XLA Ops:
  8.1 1.2 copy-done
  9.2 3.8 fusion.4
  13.1 0.5 all-gather.2.cloned.1.call-update
  13.7 6.1 all-to-all-start
  19.8 0.1 reduce.2
  20.0 0.1 select_reduce_fusion.2
  20.3 1.9 gather_fusion.1
  22.4 0.7 fusion.12
  23.1 0.7 fusion.13
  23.8 26.7 %all-to-all-done = bf16[8,128,1024]{2,1,0:T(8,128)(2,1)S(1)} async-done(((bf16[8,128,1024]{2,1,0:T(8,128)(2,1)}), bf16[8,128,1024]{2,1,0:T(8,128)(2,1)S(1)}, u32[]{:S(2)}, u32[]{:S(2)}) %all-to-all-start) | async-done | bytes 2097184 | tf_op jit(solution)/shard_map/all_to_all | solution.py:40
  50.6 8.2 all-to-all-start.2
  58.8 1.8 copy.20
  60.7 5.2 gather_fusion
  65.9 0.4 all-to-all-done.2
  66.2 6.8 all-to-all-start.3
  73.1 4.5 broadcast_select_fusion
  77.6 3.0 all-to-all-done.3
  80.6 4.6 all-to-all-start.1
  85.4 0.5 multiply_reduce_fusion.1
  85.9 29.0 %all-reduce.2.cloned.1.call-done = bf16[1024,512]{1,0:T(8,128)(2,1)} async-done(((bf16[1024,512]{1,0:T(8,128)(2,1)}), bf16[1024,512]{1,0:T(8,128)(2,1)}) %all-reduce.2.cloned.1.call-update) | async-done | bytes 1048592 | tf_op jit(solution)/shard_map/psum | solution.py:38
  114.9 1.0 multiply_convert_fusion.4
  115.9 1.2 gather_fusion.2
  117.0 0.8 broadcast_select_fusion.1
  117.8 33.6 %all-to-all-done.1 = bf16[16,16,8192]{2,1,0:T(8,128)(2,1)} async-done(((bf16[16,16,8192]{2,1,0:T(8,128)(2,1)}), bf16[16,16,8192]{2,1,0:T(8,128)(2,1)}, u32[]{:S(2)}, u32[]{:S(2)}) %all-to-all-start.1) | async-done | bytes 4194336 | tf_op jit(solution)/shard_map/all_to_all | solution.py:63
  151.4 4.9 all-to-all-start.4
  156.4 0.2 reduce-scatter.2.cloned.1.call-start
  156.6 3.2 multiply_reduce_fusion
  159.9 5.3 fusion.1
  165.2 7.0 fusion.14
  172.2 10.4 %convolution_multiply_fusion = f32[8192,512]{1,0:T(8,128)} fusion(bf16[256,8192]{1,0:T(8,128)(2,1)} %fusion.1, f32[256,512]{1,0:T(8,128)S(1)} %fusion.14, bf16[256,512]{1,0:T(8,128)(2,1)S(1)} %bitcast.38, bf16[1,1,256,512]{3,2,1,0:T(8,128)(2,1)S(1)} %copy-done.4, f32[256]{0:T(256)S(1)} %reshape.308, f32[256]{0:T(256)S(1)} %reshape.306), kind=kOutput, calls=%fused_computation.3 | convolution fusion | flops 2152595456 | bytes 22022144 | tf_op jit(solution)/shard_map/dot_general | solution.py:87
  182.7 0.7 convert_bitcast_fusion
  183.4 656.3 %reduce-scatter.2.cloned.1.call-done = f32[64,512]{1,0:T(8,128)} async-done(((f32[8192,512]{1,0:T(8,128)}), f32[64,512]{1,0:T(8,128)}) %reduce-scatter.2.cloned.1.call-update) | async-done | bytes 131088 | tf_op jit(solution)/shard_map/reduce_scatter | solution.py:86
  (42 shorter events, 1.1 us)
Async XLA Ops:
  8.0 1.2 copy-start
  8.0 106.9 %all-reduce.2.cloned.1.call-start = ((), (), s32[]{:S(2)}) async-start(), calls=%async_computation.7 | async-start | bytes 2097152 | tf_op jit(solution)/shard_map/psum | solution.py:38
  13.1 6.7 copy-start.6
  13.1 6.9 copy-start.7
  13.1 7.2 copy-start.1
  13.1 152.1 %all-gather.2.cloned.1.call-start = ((), (), s32[]{:S(2)}) async-start(), calls=%async_computation.6 | async-start | bytes 8912896 | tf_op jit(solution)/shard_map/all_gather | solution.py:81
  13.7 36.9 %all-to-all-start = ((bf16[8,128,1024]{2,1,0:T(8,128)(2,1)}), bf16[8,128,1024]{2,1,0:T(8,128)(2,1)S(1)}, u32[]{:S(2)}, u32[]{:S(2)}) async-start(bf16[8,128,1024]{2,1,0:T(8,128)(2,1)} %bitcast.37), calls=%async_computation | async-start | bytes 4194304 | tf_op jit(solution)/shard_map/all_to_all | solution.py:40
  20.3 2.0 copy-start.8
  50.5 8.3 copy-start.2
  50.6 15.7 %all-to-all-start.2 = ((bf16[16,1,16]{2,1,0:T(2,128)(2,1)}), bf16[16,1,16]{2,1,0:T(2,128)(2,1)S(1)}, u32[]{:S(2)}, u32[]{:S(2)}) async-start(bf16[16,1,16]{2,1,0:T(2,128)(2,1)} %fusion.13), calls=%async_computation.2 | async-start | bytes 16384 | tf_op jit(solution)/shard_map/all_to_all | solution.py:65
  66.2 14.3 %all-to-all-start.3 = ((bf16[16,1,16]{2,1,0:T(2,128)(2,1)}), bf16[16,1,16]{2,1,0:T(2,128)(2,1)S(1)}, u32[]{:S(2)}, u32[]{:S(2)}) async-start(bf16[16,1,16]{2,1,0:T(2,128)(2,1)} %fusion.12), calls=%async_computation.3 | async-start | bytes 16384 | tf_op jit(solution)/shard_map/all_to_all | solution.py:66
  77.6 7.8 copy-start.3
  80.6 70.8 %all-to-all-start.1 = ((bf16[16,16,8192]{2,1,0:T(8,128)(2,1)}), bf16[16,16,8192]{2,1,0:T(8,128)(2,1)}, u32[]{:S(2)}, u32[]{:S(2)}) async-start(bf16[16,16,8192]{2,1,0:T(8,128)(2,1)} %broadcast_select_fusion), calls=%async_computation.1 | async-start | bytes 8388608 | tf_op jit(solution)/shard_map/all_to_all | solution.py:63
  85.9 74.0 %copy-start.5 = (f32[8192]{0:T(1024)S(1)}, f32[8192]{0:T(1024)}, u32[]{:S(2)}) copy-start(f32[8192]{0:T(1024)} %param.13) | copy-start | bytes 98308
  151.4 20.8 %all-to-all-start.4 = ((bf16[16,16,512]{2,1,0:T(8,128)(2,1)}), bf16[16,16,512]{2,1,0:T(8,128)(2,1)S(1)}, u32[]{:S(2)}, u32[]{:S(2)}) async-start(bf16[16,16,512]{2,1,0:T(8,128)(2,1)} %broadcast_select_fusion.1), calls=%async_computation.4 | async-start | bytes 524288 | tf_op jit(solution)/shard_map/all_to_all | solution.py:64
  156.4 683.3 %reduce-scatter.2.cloned.1.call-start = ((), (), s32[]{:S(2)}) async-start(), calls=%async_computation.8 | async-start | bytes 16908288 | tf_op jit(solution)/shard_map/reduce_scatter | solution.py:86
  165.2 7.0 copy-start.4
Sparse Core Ops, SparseCore 0:
  13.2 101.6 all-reduce.1
  182.8 656.8 reduce-scatter.1
Sparse Core Ops, SparseCore 1:
  16.0 144.8 all-gather.1
where the time goes:
time: 860 us; the launch traced here: 847 us
  waiting for transfers between devices  749 us (87%)
  starting transfers between devices  30.9 us (4%)
  matrix products  21.2 us (2%)
  other arithmetic  18.1 us (2%)
  between operations  15.7 us (2%)
  local copies, waits for them, and re-layouts  11.8 us (1%)
    reduce_scatter x1, waiting for transfers between devices, on_device(): lax.psum_scatter(lax.dot_general(feature_block, slope, (((0,), (0,)), (()...  656 us
    all_to_all x1, waiting for transfers between devices, on_device(): lax.all_to_all(send_rows, 'dp', split_axis=0, concat_axis=0, tiled=True)  33.6 us
    psum x1, waiting for transfers between devices, on_device(): lax.psum(partial_value.astype(jnp.bfloat16), 'tensor').astype(jnp.float32)  29 us
    all_to_all x1, waiting for transfers between devices, on_device(): lax.all_to_all(tokens, 'tensor', split_axis=0, concat_axis=1, tiled=True)  26.7 us
  transfers between devices with their start and end apart: 8, of which 6 were waited for; matrix products, arithmetic and copies ran while one was open for 4% of the time, Pallas kernels for 0%

commit v1 on v0

v1 whole, which is shorter than its diff:
```python
import math

import jax
import jax.numpy as jnp
from jax import lax
from jax.experimental import pallas as pl
from jax.experimental.pallas import tpu as pltpu
from jax.sharding import PartitionSpec as P

EPS = 1e-06
BETA = 1.0
MESH = pl.DeviceIdType.MESH
BF = jnp.bfloat16
F32 = jnp.float32

FEAT = 1024
RB = 128
HB = RB // 2
VW = 512
CW = 256
NG = VW // CW
WIDTH = 8192
NDP = 16
SPAN = 16
CHUNK = 64


def kernel(
    x_hbm,
    rw_hbm,
    pw_hbm,
    cot_hbm,
    rg_ref,
    pg_ref,
    len_ref,
    bin_ref,
    adv_ref,
    gap_ref,
    pv_ref,
    gw_ref,
    x,
    xt,
    wr,
    wrs,
    pw,
    wp,
    wps,
    pgc,
    pb,
    ry1,
    ryd,
    ryc,
    ycb,
    qs,
    rz,
    tq,
    z1r,
    sb,
    zr1,
    zrd,
    zrc,
    zcb,
    tref,
    tpol,
    pow_s,
    pow_r,
    cr,
    ss,
    gb,
    dr0,
    hb,
    xr1,
    xrd,
    xrc,
    xcb,
    rb,
    fr,
    pvs,
    pvr,
    loc,
    msend,
    mrecv,
    asend,
    arecv,
    bsend,
    brecv,
    psend,
    precv,
    esend,
    erecv,
    fsend,
    frecv,
    dsend,
    drecv,
    zsend,
):
    d = lax.axis_index("dp")
    t = lax.axis_index("tensor")
    core = d % 2
    xx = (d // 2) % 4
    zh = d // 8
    yy = t % 4
    zl = t // 4
    rel = (xx + 4 - yy) % 4
    odd = rel % 2

    def at(dd, tt):
        return (dd, tt)

    yp = at(d, zl * 4 + (yy + 1) % 4)
    ym = at(d, zl * 4 + (yy + 3) % 4)
    zp = at(d, (1 - zl) * 4 + yy)
    xp = at((zh * 4 + (xx + 1) % 4) * 2 + core, t)
    xm = at((zh * 4 + (xx + 3) % 4) * 2 + core, t)
    cp = at(d + 1 - 2 * core, t)
    zswap = at((1 - zh) * 8 + xx * 2 + core, (1 - zl) * 4 + yy)
    same_z = zh == zl
    diag = rel == 0
    origin = jnp.logical_and(diag, same_z)
    swapper = jnp.logical_and(diag, jnp.logical_not(same_z))
    dfin = (zl * 4 + yy) * 2 + core

    def fin(k):
        return at(dfin, k * 4 + xx)

    def fin_src(s):
        return at((s * 4 + yy) * 2 + core, zh * 4 + xx)

    def fin_self(k):
        return jnp.logical_and(origin, zl == k)

    ld_rw = pltpu.make_async_copy(rw_hbm, wr, loc.at[0])
    ld_x = pltpu.make_async_copy(x_hbm, x, loc.at[1])
    ld_pw = pltpu.make_async_copy(pw_hbm, pw, loc.at[2])
    ld_cot = pltpu.make_async_copy(
        cot_hbm.at[0, 0, pl.ds(pl.multiple_of(d * SPAN, SPAN), SPAN), :], cr.at[d], loc.at[3]
    )
    ld_rw.start()
    ld_x.start()
    ld_pw.start()
    ld_cot.start()

    bar = pltpu.get_barrier_semaphore()

    def greet(dev):
        pl.semaphore_signal(bar, inc=1, device_id=dev, device_id_type=MESH)

    def greet_t(i, c):
        greet(at(d, (t + i) % 8))
        return c

    def greet_d(i, c):
        greet(at((d + i) % NDP, t))
        return c

    lax.fori_loop(1, 8, greet_t, 0)
    lax.fori_loop(1, NDP, greet_d, 0)

    @pl.when(swapper)
    def _():
        greet(zswap)

    for s in range(2):

        @pl.when(jnp.logical_not(jnp.logical_and(origin, zh == s)))
        def _():
            greet(fin_src(s))

    eye = lax.broadcasted_iota(jnp.int32, (RB, RB), 0) == lax.broadcasted_iota(
        jnp.int32, (RB, RB), 1
    )

    def to_col(row):
        return jnp.sum(
            jnp.where(eye, jnp.broadcast_to(row, (RB, RB)), 0.0), axis=1, keepdims=True
        )

    def to_row(col):
        return jnp.sum(
            jnp.where(eye, jnp.broadcast_to(col, (RB, RB)), 0.0), axis=0, keepdims=True
        )

    ld_rw.wait()
    for b in range(8):
        rows = slice(b * RB, (b + 1) * RB)
        gcol = to_col(rg_ref[b : b + 1, :])
        for g in range(NG):
            wrs[g, rows, :] = (wr[rows, g * CW : (g + 1) * CW].astype(F32) * gcol).astype(BF)
        pgc[rows, :] = to_col(pg_ref[t, b : b + 1, :])

    ld_x.wait()

    def products(u, weight):
        def step(i, c):
            rows = pl.ds(pl.multiple_of(i * CW, CW), CW)
            part = jnp.dot(x[rows, :], weight[...], preferred_element_type=F32).astype(BF)
            pb[u, i // 2, (i % 2) * 2] = part[:RB]
            pb[u, i // 2, (i % 2) * 2 + 1] = part[RB:]
            return c

        lax.fori_loop(0, 4, step, 0)

    sent = []
    ids = {}

    def copy(name, src, dst, dev):
        n = ids.setdefault(name, len(ids))
        c = pltpu.make_async_remote_copy(
            src_ref=src,
            dst_ref=dst,
            send_sem=msend.at[n],
            recv_sem=mrecv.at[n],
            device_id=dev,
            device_id_type=MESH,
        )
        c.start()
        sent.append(c)

    def arrived(name, landed):
        n = ids[name]
        pltpu.make_async_remote_copy(
            src_ref=landed,
            dst_ref=landed,
            send_sem=msend.at[n],
            recv_sem=mrecv.at[n],
            device_id=cp,
            device_id_type=MESH,
        ).wait_recv()

    y0, y1, y2, y3 = yy, (yy + 1) % 4, (yy + 2) % 4, (yy + 3) % 4

    def yu_start(u):
        n = u // 2
        copy(("y1", u, 0), pb.at[u, :, y2, 0:HB, :], ry1.at[n, 0], yp)
        copy(("y1", u, 1), pb.at[u, :, y2, HB:RB, :], ry1.at[n, 1], ym)
        copy(("yd", u, 0), pb.at[u, :, y1, HB:RB, :], ryd.at[n, 0], yp)
        copy(("yd", u, 1), pb.at[u, :, y3, 0:HB, :], ryd.at[n, 1], ym)

    def yu_combine(u):
        n = u // 2
        arrived(("y1", u, 0), ry1.at[n, 0])
        ycb[n, 0] = (pb[u, :, y1, 0:HB, :].astype(F32) + ry1[n, 0].astype(F32)).astype(BF)
        copy(("yc", u, 0), ycb.at[n, 0], ryc.at[n, 0], yp)
        arrived(("y1", u, 1), ry1.at[n, 1])
        ycb[n, 1] = (pb[u, :, y3, HB:RB, :].astype(F32) + ry1[n, 1].astype(F32)).astype(BF)
        copy(("yc", u, 1), ycb.at[n, 1], ryc.at[n, 1], ym)

    def yu_cross(u):
        n = u // 2
        for i in range(2):
            arrived(("yd", u, i), ryd.at[n, i])
        for i in range(2):
            arrived(("yc", u, i), ryc.at[n, i])

        def part(zt, lo):
            own = pb[u, zt, y0, lo : lo + HB, :].astype(F32)
            if lo == 0:
                return own + ryc[n, 0, zt].astype(F32) + ryd[n, 1, zt].astype(F32)
            return own + ryd[n, 0, zt].astype(F32) + ryc[n, 1, zt].astype(F32)

        qs[n, 0:HB, :] = part(1 - zl, 0).astype(BF)
        qs[n, HB:RB, :] = part(1 - zl, HB).astype(BF)
        copy(("yz", u), qs.at[n], rz.at[n], zp)
        tq[n, 0:HB, :] = part(zl, 0)
        tq[n, HB:RB, :] = part(zl, HB)

    def yu_finish(u, total, g):
        n = u // 2
        arrived(("yz", u), rz.at[n])
        total[:, g * CW : (g + 1) * CW] = tq[n] + rz[n].astype(F32)

    def zu_start(u):
        n = u // 2
        for o in (2, 1, 3, 0):
            copy(("z1", u, o), pb.at[u, 1 - zl, (yy + o) % 4], z1r.at[n, o], zp)

    def zu_sum(u):
        n = u // 2
        for o in (2, 1, 3):
            arrived(("z1", u, o), z1r.at[n, o])
            sb[n, o] = (pb[u, zl, (yy + o) % 4].astype(F32) + z1r[n, o].astype(F32)).astype(BF)
            if o == 2:
                copy(("zr", u, 0), sb.at[n, 2, 0:HB, :], zr1.at[n, 0], yp)
                copy(("zr", u, 1), sb.at[n, 2, HB:RB, :], zr1.at[n, 1], ym)
            elif o == 1:
                copy(("zd", u, 0), sb.at[n, 1, HB:RB, :], zrd.at[n, 0], yp)
            else:
                copy(("zd", u, 1), sb.at[n, 3, 0:HB, :], zrd.at[n, 1], ym)

    def zu_combine(u):
        n = u // 2
        arrived(("zr", u, 0), zr1.at[n, 0])
        zcb[n, 0] = (sb[n, 1, 0:HB, :].astype(F32) + zr1[n, 0].astype(F32)).astype(BF)
        copy(("zc", u, 0), zcb.at[n, 0], zrc.at[n, 0], yp)
        arrived(("zr", u, 1), zr1.at[n, 1])
        zcb[n, 1] = (sb[n, 3, HB:RB, :].astype(F32) + zr1[n, 1].astype(F32)).astype(BF)
        copy(("zc", u, 1), zcb.at[n, 1], zrc.at[n, 1], ym)

    def zu_finish(u, total, g):
        n = u // 2
        arrived(("z1", u, 0), z1r.at[n, 0])
        for i in range(2):
            arrived(("zd", u, i), zrd.at[n, i])
        for i in range(2):
            arrived(("zc", u, i), zrc.at[n, i])
        cols = slice(g * CW, (g + 1) * CW)
        own = pb[u, zl, y0].astype(F32) + z1r[n, 0].astype(F32)
        total[0:HB, cols] = own[0:HB] + zrc[n, 0].astype(F32) + zrd[n, 1].astype(F32)
        total[HB:RB, cols] = own[HB:RB] + zrd[n, 0].astype(F32) + zrc[n, 1].astype(F32)

    def a_src(q, way):
        return pl.ds(pl.multiple_of(way * 256 + (q % 2) * 128, 128), 128), q // 2

    def a_place(own, q, way):
        return wp.at[
            q // 2,
            pl.ds(pl.multiple_of(own * 512 + way * 256 + (q % 2) * 128, 128), 128),
            :,
        ]

    def a_copy(q, way, dev):
        return pltpu.make_async_remote_copy(
            src_ref=a_place(core, q, way),
            dst_ref=a_place(core, q, way),
            send_sem=asend.at[way * 4 + q],
            recv_sem=arecv.at[way * 4 + q],
            device_id=dev,
            device_id_type=MESH,
        )

    def a_swap(q, way):
        return pltpu.make_async_remote_copy(
            src_ref=pw.at[
                way * 256 + (q % 2) * 128 : way * 256 + (q % 2) * 128 + 128,
                (q // 2) * CW : (q // 2 + 1) * CW,
            ],
            dst_ref=a_place(core, q, way),
            send_sem=zsend.at[way * 4 + q],
            recv_sem=arecv.at[way * 4 + q],
            device_id=zswap,
            device_id_type=MESH,
        )

    def b_copy(own, q, way):
        return pltpu.make_async_remote_copy(
            src_ref=a_place(own, q, way),
            dst_ref=a_place(own, q, way),
            send_sem=bsend.at[way * 4 + q],
            recv_sem=brecv.at[way * 4 + q],
            device_id=cp,
            device_id_type=MESH,
        )

    def a_order(i):
        q = odd * (i % 4) + (1 - odd) * (i // 2)
        way = odd * ((i // 4 + rel // 2) % 2) + (1 - odd) * (i % 2)
        return q, way

    def a_next(way):
        return at((zh * 4 + (xx + 1 + 2 * way) % 4) * 2 + core, t)

    def a_forwards(way):
        return rel != 3 - 2 * way

    def a_step(i):
        q, way = a_order(i)

        @pl.when(jnp.logical_not(origin))
        def _():
            a_copy(q, way, xp).wait_recv()

        @pl.when(a_forwards(way))
        def _():
            a_copy(q, way, a_next(way)).start()

        b_copy(core, q, way).start()

    products(0, wrs.at[0])
    products(1, wrs.at[1])

    ld_pw.wait()

    @pl.when(origin)
    def _():
        for g in range(NG):
            wp[g, pl.ds(pl.multiple_of(core * 512, 512), 512), :] = pw[:, g * CW : (g + 1) * CW]

    pl.semaphore_wait(
        bar,
        22
        + jnp.where(swapper, 1, 0)
        + jnp.where(fin_self(0), 0, 1)
        + jnp.where(fin_self(1), 0, 1),
    )

    @pl.when(swapper)
    def _():
        for q in range(4):
            for way in range(2):
                a_swap(q, way).start()

    @pl.when(origin)
    def _():
        for i in range(8):
            a_step(i)

    yu_start(0)
    zu_start(1)

    def squares(b, c):
        rows = pl.ds(pl.multiple_of(b * RB, RB), RB)
        xb = x[rows, :].astype(F32)
        part = jnp.sum(xb * xb, axis=1, keepdims=True)
        pow_s[b] = jnp.broadcast_to(to_row(part), (8, RB))
        return c

    lax.fori_loop(0, 8, squares, 0)
    pow_r[t] = pow_s[t]

    def p_copy(peer):
        return pltpu.make_async_remote_copy(
            src_ref=pow_s.at[peer],
            dst_ref=pow_r.at[t],
            send_sem=psend.at[peer],
            recv_sem=precv.at[t],
            device_id=at(d, peer),
            device_id_type=MESH,
        )

    def p_start(i, c):
        p_copy((t + i) % 8).start()
        return c

    lax.fori_loop(1, 8, p_start, 0)

    def a_step_others(i):
        @pl.when(jnp.logical_not(origin))
        def _():
            a_step(i)

    a_step_others(0)
    yu_combine(0)
    a_step_others(1)
    zu_sum(1)
    a_step_others(2)
    a_step_others(3)
    zu_combine(1)
    a_step_others(4)
    a_step_others(5)
    yu_cross(0)

    def e_copy(peer):
        return pltpu.make_async_remote_copy(
            src_ref=cot_hbm.at[0, 0, pl.ds(pl.multiple_of(peer * SPAN, SPAN), SPAN), :],
            dst_ref=cr.at[d],
            send_sem=esend.at[peer],
            recv_sem=erecv.at[d],
            device_id=at(peer, t),
            device_id_type=MESH,
        )

    def e_start(i, c):
        e_copy((d + i) % NDP).start()
        return c

    def policy(g):
        for way in range(2):
            for q in (2 * g, 2 * g + 1):
                b_copy(1 - core, q, way).wait_recv()
        for b in range(8):
            rows = slice(b * RB, (b + 1) * RB)
            wps[g, rows, :] = (wp[g, rows, :].astype(F32) * pgc[rows, :]).astype(BF)
        products(2 + g, wps.at[g])

    policy(0)
    yu_start(2)
    a_step_others(6)
    a_step_others(7)
    lax.fori_loop(1, NDP, e_start, 0)
    policy(1)
    zu_start(3)
    zu_finish(1, tref, 1)
    yu_finish(0, tref, 0)

    def turn(i, c):
        cols = pl.ds(pl.multiple_of(i * CW, CW), CW)
        xt[cols, :] = x[:, cols].T
        return c

    lax.fori_loop(0, 4, turn, 0)
    yu_combine(2)

    row = lax.broadcasted_iota(jnp.int32, (RB, 1), 0)
    slot = jnp.zeros((RB, 1), jnp.int32)
    length = jnp.ones((RB, 1), F32)
    advantage = jnp.zeros((RB, 1), F32)
    start = jnp.int32(0)
    for s in range(16):
        n = len_ref[0, 0, s]
        inside = jnp.logical_and(row >= start, row < start + n)
        slot = jnp.where(inside, row - start + bin_ref[0, 0, s] * SPAN, slot)
        length = jnp.where(inside, n.astype(F32), length)
        advantage = jnp.where(inside, adv_ref[0, 0, s], advantage)
        start = start + n
    importance = jnp.minimum(jnp.exp(to_col(gap_ref[...])), 2.0)
    coef_adv = (advantage * importance / length).astype(BF).astype(F32)
    coef_pull = (BETA / length).astype(BF).astype(F32)
    pick = (
        jnp.broadcast_to(slot, (RB, NDP * SPAN))
        == lax.broadcasted_iota(jnp.int32, (RB, NDP * SPAN), 1)
    ).astype(BF)
    slot_row = to_row(slot.astype(F32))
    place = (
        lax.broadcasted_iota(jnp.int32, (NDP * SPAN, RB), 0).astype(F32)
        == jnp.broadcast_to(slot_row, (NDP * SPAN, RB))
    ).astype(BF)

    def p_wait(i, c):
        p = (t + i) % 8
        pltpu.make_async_remote_copy(
            src_ref=pow_r.at[p],
            dst_ref=pow_r.at[p],
            send_sem=psend.at[p],
            recv_sem=precv.at[p],
            device_id=at(d, p),
            device_id_type=MESH,
        ).wait_recv()
        return c

    lax.fori_loop(1, 8, p_wait, 0)
    power = pow_r[0]
    for k in range(1, 8):
        power = power + pow_r[k]
    scale = to_col(lax.rsqrt(power[0:1, :] * (1.0 / WIDTH) + EPS))

    zu_sum(3)
    yu_cross(2)
    zu_combine(3)

    ld_cot.wait()

    def e_wait(i, c):
        p = (d + i) % NDP
        pltpu.make_async_remote_copy(
            src_ref=cr.at[p],
            dst_ref=cr.at[p],
            send_sem=esend.at[p],
            recv_sem=erecv.at[p],
            device_id=at(p, t),
            device_id_type=MESH,
        ).wait_recv()
        return c

    lax.fori_loop(1, NDP, e_wait, 0)

    def slopes(g):
        cols = slice(g * CW, (g + 1) * CW)
        upstream = jnp.dot(
            pick, cr[:, :, cols].reshape(NDP * SPAN, CW), preferred_element_type=F32
        )
        values = tpol[:, cols] * scale
        ref_values = (tref[:, cols] * scale).astype(BF).astype(F32)
        slope = coef_adv * upstream + coef_pull * (values - ref_values)
        ss[g, zl, y0] = (slope * scale).astype(BF)
        mine = ss.at[g, zl, y0]
        copy(("cz", g), mine, mine, zp)
        copy(("cp", g), mine, mine, yp)
        copy(("cm", g), mine, mine, ym)
        out = jnp.dot(place, values.astype(BF), preferred_element_type=F32).astype(BF)
        pvs[:, :, cols] = out.reshape(NDP, SPAN, CW)

    def spread(g):
        oz = 1 - zl
        arrived(("cz", g), ss.at[g, oz, y0])
        block = ss.at[g, oz, y0]
        copy(("czp", g), block, block, yp)
        copy(("czm", g), block, block, ym)
        arrived(("cp", g), ss.at[g, zl, y3])
        half = ss.at[g, zl, y3, 0:HB, :]
        copy(("chp", g), half, half, yp)
        arrived(("cm", g), ss.at[g, zl, y1])
        half = ss.at[g, zl, y1, HB:RB, :]
        copy(("chm", g), half, half, ym)

    def spread_far(g):
        arrived(("chp", g), ss.at[g, zl, y2, 0:HB, :])
        arrived(("chm", g), ss.at[g, zl, y2, HB:RB, :])
        block = ss.at[g, zl, y2]
        copy(("czz", g), block, block, zp)

    def spread_end(g):
        oz = 1 - zl
        arrived(("czp", g), ss.at[g, oz, y3])
        arrived(("czm", g), ss.at[g, oz, y1])
        arrived(("czz", g), ss.at[g, oz, y2])

    factor = 1.0 / math.sqrt(2048.0)

    def gradient(g, half):
        def step(i, c):
            base = pl.multiple_of((half * 2 + i) * CW, CW)
            rows = pl.ds(base, CW)
            part = jnp.dot(
                xt[rows, :], ss[g].reshape(FEAT, CW), preferred_element_type=F32
            )
            part = (part * (pgc[rows, :] * factor)).astype(BF)
            gb[g, half, pl.ds(pl.multiple_of(i * 4, 4), 4)] = part.reshape(4, CHUNK, CW)
            return c

        lax.fori_loop(0, 2, step, 0)

    def reduce_core(g):
        gradient(g, 1 - core)
        copy(("d0", g), gb.at[g, 1 - core], dr0.at[g], cp)
        gradient(g, core)

    x0, x1, x2, x3 = xx, (xx + 1) % 4, (xx + 2) % 4, (xx + 3) % 4

    def reduce_x(g):
        arrived(("d0", g), dr0.at[g])
        hb[g] = (gb[g, core].astype(F32) + dr0[g].astype(F32)).astype(BF)
        copy(("x1", g, 0), hb.at[g, x2], xr1.at[g, 0], xp)
        copy(("x1", g, 1), hb.at[g, 4 + x2], xr1.at[g, 1], xm)
        copy(("xd", g, 0), hb.at[g, 4 + x1], xrd.at[g, 0], xp)
        copy(("xd", g, 1), hb.at[g, x3], xrd.at[g, 1], xm)

    def combine_x(g):
        arrived(("x1", g, 0), xr1.at[g, 0])
        xcb[g, 0] = (hb[g, x1].astype(F32) + xr1[g, 0].astype(F32)).astype(BF)
        copy(("xc", g, 0), xcb.at[g, 0], xrc.at[g, 0], xp)
        arrived(("x1", g, 1), xr1.at[g, 1])
        xcb[g, 1] = (hb[g, 4 + x3].astype(F32) + xr1[g, 1].astype(F32)).astype(BF)
        copy(("xc", g, 1), xcb.at[g, 1], xrc.at[g, 1], xm)

    def d_copy(g, k):
        return pltpu.make_async_remote_copy(
            src_ref=rb.at[g, k],
            dst_ref=fr.at[g, zh],
            send_sem=dsend.at[g * 2 + k],
            recv_sem=drecv.at[g * 2 + zh],
            device_id=fin(k),
            device_id_type=MESH,
        )

    def to_owner(g):
        for i in range(2):
            arrived(("xd", g, i), xrd.at[g, i])
        for i in range(2):
            arrived(("xc", g, i), xrc.at[g, i])
        rb[g, 0] = (
            hb[g, x0].astype(F32) + xrc[g, 0].astype(F32) + xrd[g, 1].astype(F32)
        ).astype(BF)
        rb[g, 1] = (
            hb[g, 4 + x0].astype(F32) + xrd[g, 0].astype(F32) + xrc[g, 1].astype(F32)
        ).astype(BF)
        for k in range(2):

            @pl.when(fin_self(k))
            def _():
                fr[g, zh] = rb[g, k]

            @pl.when(jnp.logical_not(fin_self(k)))
            def _():
                d_copy(g, k).start()

    def finish(g):
        for s in range(2):

            @pl.when(jnp.logical_not(jnp.logical_and(origin, zh == s)))
            def _():
                pltpu.make_async_remote_copy(
                    src_ref=fr.at[g, s],
                    dst_ref=fr.at[g, s],
                    send_sem=dsend.at[g * 2],
                    recv_sem=drecv.at[g * 2 + s],
                    device_id=cp,
                    device_id_type=MESH,
                ).wait_recv()

        gw_ref[:, g * CW : (g + 1) * CW] = fr[g, 0].astype(F32) + fr[g, 1].astype(F32)

    def f_copy(peer):
        return pltpu.make_async_remote_copy(
            src_ref=pvs.at[peer],
            dst_ref=pvr.at[d],
            send_sem=fsend.at[peer],
            recv_sem=frecv.at[d],
            device_id=at(peer, t),
            device_id_type=MESH,
        )

    def f_start(i, c):
        f_copy((d + i) % NDP).start()
        return c

    def f_wait(i, c):
        p = (d + i) % NDP
        pltpu.make_async_remote_copy(
            src_ref=pvr.at[p],
            dst_ref=pvr.at[p],
            send_sem=fsend.at[p],
            recv_sem=frecv.at[p],
            device_id=at(p, t),
            device_id_type=MESH,
        ).wait_recv()
        return c

    yu_finish(2, tpol, 0)
    slopes(0)
    zu_finish(3, tpol, 1)
    slopes(1)
    spread(0)
    pvr[d] = pvs[d]
    lax.fori_loop(1, NDP, f_start, 0)
    spread(1)
    spread_far(0)
    spread_far(1)
    spread_end(0)
    reduce_core(0)
    reduce_x(0)
    spread_end(1)
    reduce_core(1)
    combine_x(0)
    reduce_x(1)
    to_owner(0)
    combine_x(1)
    lax.fori_loop(1, NDP, f_wait, 0)
    pv_ref[0, 0] = pvr[...].reshape(NDP * SPAN, VW)
    to_owner(1)
    finish(0)
    finish(1)

    for c in sent:
        c.wait_send()

    @pl.when(swapper)
    def _():
        for q in range(4):
            for way in range(2):
                a_swap(q, way).wait_send()

    for way in range(2):

        @pl.when(a_forwards(way))
        def _():
            for q in range(4):
                a_copy(q, way, a_next(way)).wait_send()

        for q in range(4):
            b_copy(core, q, way).wait_send()

    def p_done(i, c):
        p_copy((t + i) % 8).wait_send()
        return c

    def ef_done(i, c):
        e_copy((d + i) % NDP).wait_send()
        f_copy((d + i) % NDP).wait_send()
        return c

    lax.fori_loop(1, 8, p_done, 0)
    lax.fori_loop(1, NDP, ef_done, 0)
    for g in range(NG):
        for k in range(2):

            @pl.when(jnp.logical_not(fin_self(k)))
            def _():
                d_copy(g, k).wait_send()


def on_device(
    tokens,
    ref_gain,
    ref_weight,
    pol_gain,
    pol_weight,
    lengths,
    bins,
    advantage,
    logprob_gap,
    cotangent,
):
    any_spec = pl.BlockSpec(memory_space=pl.ANY)
    vmem = pl.BlockSpec(memory_space=pltpu.VMEM)
    smem = pl.BlockSpec(memory_space=pltpu.SMEM)
    dma = pltpu.SemaphoreType.DMA

    def buf(*shape, dtype=BF):
        return pltpu.VMEM(shape, dtype)

    return pl.pallas_call(
        kernel,
        out_shape=(
            jax.ShapeDtypeStruct(cotangent.shape, BF),
            jax.ShapeDtypeStruct((CHUNK, VW), F32),
        ),
        in_specs=[any_spec] * 4 + [vmem, vmem, smem, smem, smem, vmem],
        out_specs=(vmem, vmem),
        scratch_shapes=[
            buf(1024, FEAT),
            buf(FEAT, 1024),
            buf(FEAT, VW),
            buf(NG, FEAT, CW),
            buf(512, VW),
            buf(NG, FEAT, CW),
            buf(NG, FEAT, CW),
            buf(FEAT, 1, dtype=F32),
            buf(4, 2, 4, RB, CW),
            buf(2, 2, 2, HB, CW),
            buf(2, 2, 2, HB, CW),
            buf(2, 2, 2, HB, CW),
            buf(2, 2, 2, HB, CW),
            buf(2, RB, CW),
            buf(2, RB, CW),
            buf(2, RB, CW, dtype=F32),
            buf(2, 4, RB, CW),
            buf(2, 4, RB, CW),
            buf(2, 2, HB, CW),
            buf(2, 2, HB, CW),
            buf(2, 2, HB, CW),
            buf(2, 2, HB, CW),
            buf(RB, VW, dtype=F32),
            buf(RB, VW, dtype=F32),
            buf(8, 8, RB, dtype=F32),
            buf(8, 8, RB, dtype=F32),
            buf(NDP, SPAN, VW),
            buf(NG, 2, 4, RB, CW),
            buf(NG, 2, 8, CHUNK, CW),
            buf(NG, 8, CHUNK, CW),
            buf(NG, 8, CHUNK, CW),
            buf(NG, 2, CHUNK, CW),
            buf(NG, 2, CHUNK, CW),
            buf(NG, 2, CHUNK, CW),
            buf(NG, 2, CHUNK, CW),
            buf(NG, 2, CHUNK, CW),
            buf(NG, 2, CHUNK, CW),
            buf(NDP, SPAN, VW),
            buf(NDP, SPAN, VW),
            dma((4,)),
            dma((64,)),
            dma((64,)),
            dma((8,)),
            dma((8,)),
            dma((8,)),
            dma((8,)),
            dma((8,)),
            dma((8,)),
            dma((NDP,)),
            dma((NDP,)),
            dma((NDP,)),
            dma((NDP,)),
            dma((4,)),
            dma((4,)),
            dma((8,)),
        ],
        compiler_params=pltpu.CompilerParams(collective_id=0, has_side_effects=True),
    )(
        tokens,
        ref_weight,
        pol_weight,
        cotangent,
        ref_gain.reshape(8, RB),
        pol_gain.reshape(8, 8, RB),
        lengths,
        bins,
        advantage,
        logprob_gap.reshape(1, RB),
    )


def solution(mesh):
    in_specs = (
        P("dp", "tensor"),
        P("tensor"),
        P("tensor", None),
        P(),
        P("dp", None),
        P("dp", "tensor", None),
        P("dp", "tensor", None),
        P("dp", "tensor", None),
        P(("dp", "tensor")),
        P("dp", "tensor", None, None),
    )
    out_specs = (P("dp", "tensor", None, None), P(("dp", "tensor"), None))
    return jax.shard_map(
        on_device, mesh=mesh, in_specs=in_specs, out_specs=out_specs, check_vma=False
    )
```

time: 860 us -> 86.7 us (0.10); the launches traced: 847 us -> 85.3 us
  waiting for transfers between devices: 749 us -> 0 us
  Pallas kernels: 0 us -> 81.4 us
  starting transfers between devices: 30.9 us -> 0 us
  matrix products: 21.2 us -> 0 us
  other arithmetic: 18.1 us -> 0 us
  between operations: 15.7 us -> 0.64 us
    reduce_scatter x1 -> x0, waiting for transfers between devices: 656 us -> none  [on_device(): lax.psum_scatter(lax.dot_general(feature_block, slope, (((0,), (0,)), (()...]
    pallas_call x0 -> x1, Pallas kernels: none -> 81.4 us  [on_device(): pl.pallas_call(kernel, out_shape=(jax.ShapeDtypeStruct(cotangent.shape, B...]
    all_to_all x5 -> x0, waiting for transfers between devices: 63.7 us -> none  [the longest x1 33.6 us: on_device(): lax.all_to_all(send_rows, 'dp', split_axis=0, concat_axis=0, tiled=True)]
    all_to_all x5 -> x0, starting transfers between devices: 30.6 us -> none  [the longest x1 8.21 us: on_device(): lax.all_to_all(coef_adv, 'dp', split_axis=0, concat_axis=0, tiled=True)]
    psum x1 -> x0, waiting for transfers between devices: 29 us -> none  [on_device(): lax.psum(partial_value.astype(jnp.bfloat16), 'tensor').astype(jnp.float32)]
    dot_general x3 -> x0, matrix products: 21.2 us -> none  [the longest x1 10.4 us: on_device(): lax.dot_general(feature_block, slope, (((0,), (0,)), ((), ())), preferred...]
  transfers between devices with their start and end apart: 8 -> 0, of which waited for: 6 -> 0; matrix products, arithmetic and copies ran while one was open for 4% -> 0% of each run, Pallas kernels for 0% -> 0%
where the time goes in v1:
time: 86.7 us; the launch traced here: 85.3 us
  Pallas kernels  81.4 us (94%)
  local copies, waits for them, and re-layouts  3.24 us (4%)
    pallas_call x1, Pallas kernels, on_device(): pl.pallas_call(kernel, out_shape=(jax.ShapeDtypeStruct(cotangent.shape, B...  81.4 us
    unnamed x2, local copies, waits for them, and re-layouts  3.24 us

profile of v1, /device:TPU:24, one launch (start us, length us, event | category | flops | bytes accessed | tf_op | source)
XLA Modules:
  0.0 85.3 jit_solution(13650051049504695601)
XLA Ops:
  0.6 81.4 %shard_map.113 = (bf16[1,1,256,512]{3,2,1,0:T(8,128)(2,1)}, f32[64,512]{1,0:T(8,128)}) custom-call(bf16[1024,1024]{1,0:T(8,128)(2,1)} %x_hbm.1, bf16[1024,512]{1,0:T(8,128)(2,1)} %rw_hbm.1, bf16[512,512]{1,0:T(8,128)(2,1)} %pw_hbm.1, bf16[1,1,256,512]{3,2,1,0:T(8,128)(2,1)} %cot_hbm.1, f32[8,128]{1,0:T(8,128)} %bitcast.4, f32[8,8,128]{2,1,0:T(8,128)} %bitcast.3, ...), custom_call_target="tpu_custom_call" | custom-call | tf_op jit(solution)/shard_map/pallas_call | solution.py:791
  82.1 1.7 %copy.14 = bf16[1,1,256,512]{3,2,1,0:T(8,128)(2,1)} copy(bf16[1,1,256,512]{3,2,1,0:T(8,128)(2,1)} %get-tuple-element.4) | data formatting | bytes 524288
  83.7 1.6 %copy.15 = f32[64,512]{1,0:T(8,128)} copy(f32[64,512]{1,0:T(8,128)} %get-tuple-element.5) | data formatting | bytes 262144

commit v2 on v1

v2 whole, which is shorter than its diff:
```python
import math

import jax
import jax.numpy as jnp
from jax import lax
from jax.experimental import pallas as pl
from jax.experimental.pallas import tpu as pltpu
from jax.sharding import PartitionSpec as P

EPS = 1e-06
BETA = 1.0
MESH = pl.DeviceIdType.MESH
BF = jnp.bfloat16
F32 = jnp.float32

FEAT = 1024
RB = 128
HB = RB // 2
VW = 512
CW = 256
NG = VW // CW
WIDTH = 8192
NDP = 16
SPAN = 16
AP = 64
MODES = "yzee"
CHUNK = 64


def kernel(
    x_hbm,
    rw_hbm,
    pw_hbm,
    cot_hbm,
    rg_ref,
    pg_ref,
    len_ref,
    bin_ref,
    adv_ref,
    gap_ref,
    pv_ref,
    gw_ref,
    x,
    xt,
    wr,
    wrs,
    pw,
    wp,
    wps,
    pgc,
    pb,
    ry1,
    ryd,
    ryc,
    re,
    ycb,
    qs,
    rz,
    tq,
    z1r,
    sb,
    zr1,
    zrd,
    zrc,
    zcb,
    tref,
    tpol,
    pow_s,
    pow_r,
    cr,
    ss,
    gb,
    dr0,
    hb,
    xr,
    rb,
    fr,
    pvs,
    pvr,
    loc,
    msend,
    mrecv,
    asend,
    arecv,
    psend,
    precv,
    esend,
    erecv,
    fsend,
    frecv,
    dsend,
    drecv,
):
    d = lax.axis_index("dp")
    t = lax.axis_index("tensor")
    core = d % 2
    xx = (d // 2) % 4
    zh = d // 8
    yy = t % 4
    zl = t // 4

    def at(dd, tt):
        return (dd, tt)

    yp = at(d, zl * 4 + (yy + 1) % 4)
    ym = at(d, zl * 4 + (yy + 3) % 4)
    yf = at(d, zl * 4 + (yy + 2) % 4)
    zp = at(d, (1 - zl) * 4 + yy)
    xp = at((zh * 4 + (xx + 1) % 4) * 2 + core, t)
    xm = at((zh * 4 + (xx + 3) % 4) * 2 + core, t)
    xf = at((zh * 4 + (xx + 2) % 4) * 2 + core, t)
    cp = at(d + 1 - 2 * core, t)
    same_z = zh == zl
    origin = jnp.logical_and(xx == yy, same_z)
    dfin = (zl * 4 + yy) * 2 + core

    def fin(k):
        return at(dfin, k * 4 + xx)

    def fin_src(s):
        return at((s * 4 + yy) * 2 + core, zh * 4 + xx)

    def fin_self(k):
        return jnp.logical_and(origin, zl == k)

    ld_rw = pltpu.make_async_copy(rw_hbm, wr, loc.at[0])
    ld_x = pltpu.make_async_copy(x_hbm, x, loc.at[1])
    ld_pw = pltpu.make_async_copy(pw_hbm, pw, loc.at[2])
    ld_cot = pltpu.make_async_copy(
        cot_hbm.at[0, 0, pl.ds(pl.multiple_of(d * SPAN, SPAN), SPAN), :], cr.at[d], loc.at[3]
    )
    ld_rw.start()
    ld_x.start()
    ld_pw.start()
    ld_cot.start()

    bar = pltpu.get_barrier_semaphore()

    def greet(dev):
        pl.semaphore_signal(bar, inc=1, device_id=dev, device_id_type=MESH)

    def greet_t(i, c):
        greet(at(d, (t + i) % 8))
        return c

    def greet_d(i, c):
        greet(at((d + i) % NDP, t))
        return c

    lax.fori_loop(1, 8, greet_t, 0)
    lax.fori_loop(1, NDP, greet_d, 0)

    def greet_w(i, c):
        @pl.when(jnp.logical_or(d // 2 != t, i != t))
        def _():
            greet(at(2 * t + core, i))

        return c

    lax.fori_loop(0, 8, greet_w, 0)

    for s in range(2):

        @pl.when(jnp.logical_not(jnp.logical_and(origin, zh == s)))
        def _():
            greet(fin_src(s))

    eye = lax.broadcasted_iota(jnp.int32, (RB, RB), 0) == lax.broadcasted_iota(
        jnp.int32, (RB, RB), 1
    )

    def to_col(row):
        return jnp.sum(
            jnp.where(eye, jnp.broadcast_to(row, (RB, RB)), 0.0), axis=1, keepdims=True
        )

    def to_row(col):
        return jnp.sum(
            jnp.where(eye, jnp.broadcast_to(col, (RB, RB)), 0.0), axis=0, keepdims=True
        )

    ld_rw.wait()
    for b in range(8):
        rows = slice(b * RB, (b + 1) * RB)
        gcol = to_col(rg_ref[b : b + 1, :])
        for g in range(NG):
            wrs[g, rows, :] = (wr[rows, g * CW : (g + 1) * CW].astype(F32) * gcol).astype(BF)
        pgc[rows, :] = to_col(pg_ref[t, b : b + 1, :])

    ld_x.wait()

    def products(u, weight):
        def step(i, c):
            rows = pl.ds(pl.multiple_of(i * CW, CW), CW)
            part = jnp.dot(x[rows, :], weight[...], preferred_element_type=F32).astype(BF)
            pb[u, i // 2, (i % 2) * 2] = part[:RB]
            pb[u, i // 2, (i % 2) * 2 + 1] = part[RB:]
            return c

        lax.fori_loop(0, 4, step, 0)

    sent = []
    ids = {}

    def copy(name, src, dst, dev):
        n = ids.setdefault(name, len(ids))
        c = pltpu.make_async_remote_copy(
            src_ref=src,
            dst_ref=dst,
            send_sem=msend.at[n],
            recv_sem=mrecv.at[n],
            device_id=dev,
            device_id_type=MESH,
        )
        c.start()
        sent.append(c)

    def arrived(name, landed):
        n = ids[name]
        pltpu.make_async_remote_copy(
            src_ref=landed,
            dst_ref=landed,
            send_sem=msend.at[n],
            recv_sem=mrecv.at[n],
            device_id=cp,
            device_id_type=MESH,
        ).wait_recv()

    y0, y1, y2, y3 = yy, (yy + 1) % 4, (yy + 2) % 4, (yy + 3) % 4

    def start_y(u):
        n = u
        copy(("y1", u, 0), pb.at[u, :, y2, 0:HB, :], ry1.at[n, 0], yp)
        copy(("y1", u, 1), pb.at[u, :, y2, HB:RB, :], ry1.at[n, 1], ym)
        copy(("yd", u, 0), pb.at[u, :, y1, HB:RB, :], ryd.at[n, 0], yp)
        copy(("yd", u, 1), pb.at[u, :, y3, 0:HB, :], ryd.at[n, 1], ym)

    def combine_y(u):
        n = u
        arrived(("y1", u, 0), ry1.at[n, 0])
        ycb[n, 0] = (pb[u, :, y1, 0:HB, :].astype(F32) + ry1[n, 0].astype(F32)).astype(BF)
        copy(("yc", u, 0), ycb.at[n, 0], ryc.at[n, 0], yp)
        arrived(("y1", u, 1), ry1.at[n, 1])
        ycb[n, 1] = (pb[u, :, y3, HB:RB, :].astype(F32) + ry1[n, 1].astype(F32)).astype(BF)
        copy(("yc", u, 1), ycb.at[n, 1], ryc.at[n, 1], ym)

    def cross_y(u):
        n = u
        for i in range(2):
            arrived(("yd", u, i), ryd.at[n, i])
        for i in range(2):
            arrived(("yc", u, i), ryc.at[n, i])

        def part(zt, lo):
            own = pb[u, zt, y0, lo : lo + HB, :].astype(F32)
            if lo == 0:
                return own + ryc[n, 0, zt].astype(F32) + ryd[n, 1, zt].astype(F32)
            return own + ryd[n, 0, zt].astype(F32) + ryc[n, 1, zt].astype(F32)

        qs[n, 0:HB, :] = part(1 - zl, 0).astype(BF)
        qs[n, HB:RB, :] = part(1 - zl, HB).astype(BF)
        copy(("yz", u), qs.at[n], rz.at[n], zp)
        tq[n, 0:HB, :] = part(zl, 0)
        tq[n, HB:RB, :] = part(zl, HB)

    def finish_y(u, total, g):
        n = u
        arrived(("yz", u), rz.at[n])
        total[:, g * CW : (g + 1) * CW] = tq[n] + rz[n].astype(F32)

    def start_z(u):
        n = u
        for o in (2, 1, 3, 0):
            copy(("z1", u, o), pb.at[u, 1 - zl, (yy + o) % 4], z1r.at[n, o], zp)

    def sum_z(u):
        n = u
        for o in (2, 1, 3):
            arrived(("z1", u, o), z1r.at[n, o])
            sb[n, o] = (pb[u, zl, (yy + o) % 4].astype(F32) + z1r[n, o].astype(F32)).astype(BF)
            if o == 2:
                copy(("zr", u, 0), sb.at[n, 2, 0:HB, :], zr1.at[n, 0], yp)
                copy(("zr", u, 1), sb.at[n, 2, HB:RB, :], zr1.at[n, 1], ym)
            elif o == 1:
                copy(("zd", u, 0), sb.at[n, 1, HB:RB, :], zrd.at[n, 0], yp)
            else:
                copy(("zd", u, 1), sb.at[n, 3, 0:HB, :], zrd.at[n, 1], ym)

    def combine_z(u):
        n = u
        arrived(("zr", u, 0), zr1.at[n, 0])
        zcb[n, 0] = (sb[n, 1, 0:HB, :].astype(F32) + zr1[n, 0].astype(F32)).astype(BF)
        copy(("zc", u, 0), zcb.at[n, 0], zrc.at[n, 0], yp)
        arrived(("zr", u, 1), zr1.at[n, 1])
        zcb[n, 1] = (sb[n, 3, HB:RB, :].astype(F32) + zr1[n, 1].astype(F32)).astype(BF)
        copy(("zc", u, 1), zcb.at[n, 1], zrc.at[n, 1], ym)

    def finish_z(u, total, g):
        n = u
        arrived(("z1", u, 0), z1r.at[n, 0])
        for i in range(2):
            arrived(("zd", u, i), zrd.at[n, i])
        for i in range(2):
            arrived(("zc", u, i), zrc.at[n, i])
        cols = slice(g * CW, (g + 1) * CW)
        own = pb[u, zl, y0].astype(F32) + z1r[n, 0].astype(F32)
        total[0:HB, cols] = own[0:HB] + zrc[n, 0].astype(F32) + zrd[n, 1].astype(F32)
        total[HB:RB, cols] = own[HB:RB] + zrd[n, 0].astype(F32) + zrc[n, 1].astype(F32)

    def start_e(u):
        copy(("e", u, 2), pb.at[u, :, y2], re.at[u, 2], yf)
        copy(("e", u, 0), pb.at[u, :, y1], re.at[u, 0], yp)
        copy(("e", u, 1), pb.at[u, :, y3], re.at[u, 1], ym)

    def none(u):
        pass

    def cross_e(u):
        for i in range(3):
            arrived(("e", u, i), re.at[u, i])

        def part(zt):
            whole = pb[u, zt, y0].astype(F32)
            for i in range(3):
                whole = whole + re[u, i, zt].astype(F32)
            return whole

        qs[u] = part(1 - zl).astype(BF)
        copy(("yz", u), qs.at[u], rz.at[u], zp)
        tq[u] = part(zl)

    def unit(u):
        if MODES[u] == "e":
            return start_e, none, cross_e, finish_y
        return (start_y, combine_y, cross_y, finish_y) if MODES[u] == "y" else (start_z, sum_z, combine_z, finish_z)

    def start(u):
        unit(u)[0](u)

    def second(u):
        unit(u)[1](u)

    def third(u):
        unit(u)[2](u)

    def finish_unit(u):
        unit(u)[3](u, (tref, tref, tpol, tpol)[u], u % 2)

    def w_copy(g, i):
        rank = (d // 2 + t + i) % 8
        return pltpu.make_async_remote_copy(
            src_ref=pw.at[
                pl.ds(pl.multiple_of(t * AP, AP), AP), g * CW : (g + 1) * CW
            ],
            dst_ref=wp.at[g, pl.ds(pl.multiple_of(core * 512 + t * AP, AP), AP), :],
            send_sem=asend.at[g * 8 + rank],
            recv_sem=arecv.at[g * 8 + t],
            device_id=at(rank * 2 + core, d // 2),
            device_id_type=MESH,
        )

    def w_remote(i):
        return jnp.logical_or(d // 2 != t, (d // 2 + t + i) % 8 != d // 2)

    def w_start(g):
        def step(i, c):
            @pl.when(w_remote(i))
            def _():
                w_copy(g, i).start()

            return c

        lax.fori_loop(0, 8, step, 0)

    def w_sent(g):
        def step(i, c):
            @pl.when(w_remote(i))
            def _():
                w_copy(g, i).wait_send()

            return c

        lax.fori_loop(0, 8, step, 0)

    def w_share(g):
        def step(i, c):
            part = wp.at[g, pl.ds(pl.multiple_of(core * 512 + i * AP, AP), AP), :]

            @pl.when(jnp.logical_or(d // 2 != t, i != t))
            def _():
                pltpu.make_async_remote_copy(
                    src_ref=part,
                    dst_ref=part,
                    send_sem=asend.at[g * 8 + i],
                    recv_sem=arecv.at[g * 8 + i],
                    device_id=cp,
                    device_id_type=MESH,
                ).wait_recv()

            return c

        lax.fori_loop(0, 8, step, 0)
        mine = wp.at[g, pl.ds(pl.multiple_of(core * 512, 512), 512), :]
        copy(("w", g), mine, mine, cp)

    products(0, wrs.at[0])
    products(1, wrs.at[1])

    ld_pw.wait()

    @pl.when(d // 2 == t)
    def _():
        for g in range(NG):
            wp[g, pl.ds(pl.multiple_of(core * 512 + t * AP, AP), AP), :] = pw[
                pl.ds(pl.multiple_of(t * AP, AP), AP), g * CW : (g + 1) * CW
            ]

    pl.semaphore_wait(
        bar,
        30
        - jnp.where(d // 2 == t, 1, 0)
        + jnp.where(fin_self(0), 0, 1)
        + jnp.where(fin_self(1), 0, 1),
    )


    w_start(0)
    start(0)
    w_start(1)
    start(1)

    def squares(b, c):
        rows = pl.ds(pl.multiple_of(b * RB, RB), RB)
        xb = x[rows, :].astype(F32)
        part = jnp.sum(xb * xb, axis=1, keepdims=True)
        pow_s[b] = jnp.broadcast_to(to_row(part), (8, RB))
        return c

    lax.fori_loop(0, 8, squares, 0)
    pow_r[t] = pow_s[t]

    def p_copy(peer):
        return pltpu.make_async_remote_copy(
            src_ref=pow_s.at[peer],
            dst_ref=pow_r.at[t],
            send_sem=psend.at[peer],
            recv_sem=precv.at[t],
            device_id=at(d, peer),
            device_id_type=MESH,
        )

    def p_start(i, c):
        p_copy((t + i) % 8).start()
        return c

    lax.fori_loop(1, 8, p_start, 0)


    def e_copy(peer):
        return pltpu.make_async_remote_copy(
            src_ref=cot_hbm.at[0, 0, pl.ds(pl.multiple_of(peer * SPAN, SPAN), SPAN), :],
            dst_ref=cr.at[d],
            send_sem=esend.at[peer],
            recv_sem=erecv.at[d],
            device_id=at(peer, t),
            device_id_type=MESH,
        )

    def e_start(i, c):
        e_copy((d + i) % NDP).start()
        return c

    def policy(g):
        arrived(("w", g), wp.at[g, pl.ds(pl.multiple_of((1 - core) * 512, 512), 512), :])
        for b in range(8):
            rows = slice(b * RB, (b + 1) * RB)
            wps[g, rows, :] = (wp[g, rows, :].astype(F32) * pgc[rows, :]).astype(BF)
        products(2 + g, wps.at[g])

    def slopes(g):
        cols = slice(g * CW, (g + 1) * CW)
        upstream = jnp.dot(
            pick, cr[:, :, cols].reshape(NDP * SPAN, CW), preferred_element_type=F32
        )
        values = tpol[:, cols] * scale
        ref_values = (tref[:, cols] * scale).astype(BF).astype(F32)
        slope = coef_adv * upstream + coef_pull * (values - ref_values)
        ss[g, zl, y0] = (slope * scale).astype(BF)
        mine = ss.at[g, zl, y0]
        copy(("cf", g), mine, mine, yf)
        copy(("cz", g), mine, mine, zp)
        copy(("cp", g), mine, mine, yp)
        copy(("cm", g), mine, mine, ym)
        out = jnp.dot(place, values.astype(BF), preferred_element_type=F32).astype(BF)
        pvs[:, :, cols] = out.reshape(NDP, SPAN, CW)

    def spread(g):
        oz = 1 - zl
        arrived(("cz", g), ss.at[g, oz, y0])
        block = ss.at[g, oz, y0]
        copy(("czp", g), block, block, yp)
        copy(("czm", g), block, block, ym)

    def spread_far(g):
        block = ss.at[g, zl, y2]
        arrived(("cf", g), block)
        copy(("czz", g), block, block, zp)

    def spread_end(g):
        oz = 1 - zl
        arrived(("cp", g), ss.at[g, zl, y3])
        arrived(("cm", g), ss.at[g, zl, y1])
        arrived(("czp", g), ss.at[g, oz, y3])
        arrived(("czm", g), ss.at[g, oz, y1])
        arrived(("czz", g), ss.at[g, oz, y2])

    factor = 1.0 / math.sqrt(2048.0)

    def gradient(g, half):
        def step(i, c):
            base = pl.multiple_of((half * 2 + i) * CW, CW)
            rows = pl.ds(base, CW)
            part = jnp.dot(
                xt[rows, :], ss[g].reshape(FEAT, CW), preferred_element_type=F32
            )
            part = (part * (pgc[rows, :] * factor)).astype(BF)
            gb[g, half, pl.ds(pl.multiple_of(i * 4, 4), 4)] = part.reshape(4, CHUNK, CW)
            return c

        lax.fori_loop(0, 2, step, 0)

    def reduce_core(g):
        gradient(g, 1 - core)
        copy(("d0", g), gb.at[g, 1 - core], dr0.at[g], cp)
        gradient(g, core)

    x0, x1, x2, x3 = xx, (xx + 1) % 4, (xx + 2) % 4, (xx + 3) % 4

    def reduce_x(g):
        arrived(("d0", g), dr0.at[g])
        hb[g] = (gb[g, core].astype(F32) + dr0[g].astype(F32)).astype(BF)
        for i, (quarter, dev) in enumerate(((x2, xf), (x1, xp), (x3, xm))):
            for k in range(2):
                copy(("x", g, i, k), hb.at[g, 4 * k + quarter], xr.at[g, i, k], dev)

    def d_copy(g, k):
        return pltpu.make_async_remote_copy(
            src_ref=rb.at[g, k],
            dst_ref=fr.at[g, zh],
            send_sem=dsend.at[g * 2 + k],
            recv_sem=drecv.at[g * 2 + zh],
            device_id=fin(k),
            device_id_type=MESH,
        )

    def to_owner(g):
        for k in range(2):
            whole = hb[g, 4 * k + x0].astype(F32)
            for i in range(3):
                arrived(("x", g, i, k), xr.at[g, i, k])
                whole = whole + xr[g, i, k].astype(F32)
            rb[g, k] = whole.astype(BF)
        for k in range(2):

            @pl.when(fin_self(k))
            def _():
                fr[g, zh] = rb[g, k]

            @pl.when(jnp.logical_not(fin_self(k)))
            def _():
                d_copy(g, k).start()

    def finish_waits(g):
        for s in range(2):

            @pl.when(jnp.logical_not(jnp.logical_and(origin, zh == s)))
            def _():
                pltpu.make_async_remote_copy(
                    src_ref=fr.at[g, s],
                    dst_ref=fr.at[g, s],
                    send_sem=dsend.at[g * 2],
                    recv_sem=drecv.at[g * 2 + s],
                    device_id=cp,
                    device_id_type=MESH,
                ).wait_recv()

    def finish(g):
        finish_waits(g)
        gw_ref[:, g * CW : (g + 1) * CW] = fr[g, 0].astype(F32) + fr[g, 1].astype(F32)

    def f_copy(peer):
        return pltpu.make_async_remote_copy(
            src_ref=pvs.at[peer],
            dst_ref=pvr.at[d],
            send_sem=fsend.at[peer],
            recv_sem=frecv.at[d],
            device_id=at(peer, t),
            device_id_type=MESH,
        )

    def f_start(i, c):
        f_copy((d + i) % NDP).start()
        return c

    def f_wait(i, c):
        p = (d + i) % NDP
        pltpu.make_async_remote_copy(
            src_ref=pvr.at[p],
            dst_ref=pvr.at[p],
            send_sem=fsend.at[p],
            recv_sem=frecv.at[p],
            device_id=at(p, t),
            device_id_type=MESH,
        ).wait_recv()
        return c

    second(0)
    def turn(i, c):
        cols = pl.ds(pl.multiple_of(i * CW, CW), CW)
        xt[cols, :] = x[:, cols].T
        return c

    lax.fori_loop(0, 4, turn, 0)
    row = lax.broadcasted_iota(jnp.int32, (RB, 1), 0)
    slot = jnp.zeros((RB, 1), jnp.int32)
    length = jnp.ones((RB, 1), F32)
    advantage = jnp.zeros((RB, 1), F32)
    first = jnp.int32(0)
    for s in range(16):
        n = len_ref[0, 0, s]
        inside = jnp.logical_and(row >= first, row < first + n)
        slot = jnp.where(inside, row - first + bin_ref[0, 0, s] * SPAN, slot)
        length = jnp.where(inside, n.astype(F32), length)
        advantage = jnp.where(inside, adv_ref[0, 0, s], advantage)
        first = first + n
    importance = jnp.minimum(jnp.exp(to_col(gap_ref[...])), 2.0)
    coef_adv = (advantage * importance / length).astype(BF).astype(F32)
    coef_pull = (BETA / length).astype(BF).astype(F32)
    pick = (
        jnp.broadcast_to(slot, (RB, NDP * SPAN))
        == lax.broadcasted_iota(jnp.int32, (RB, NDP * SPAN), 1)
    ).astype(BF)
    slot_row = to_row(slot.astype(F32))
    place = (
        lax.broadcasted_iota(jnp.int32, (NDP * SPAN, RB), 0).astype(F32)
        == jnp.broadcast_to(slot_row, (NDP * SPAN, RB))
    ).astype(BF)

    w_share(0)
    policy(0)
    start(2)
    third(0)
    second(1)
    lax.fori_loop(1, NDP, e_start, 0)
    w_share(1)
    policy(1)
    start(3)
    second(2)
    finish_unit(0)
    third(1)
    third(2)

    def p_wait(i, c):
        p = (t + i) % 8
        pltpu.make_async_remote_copy(
            src_ref=pow_r.at[p],
            dst_ref=pow_r.at[p],
            send_sem=psend.at[p],
            recv_sem=precv.at[p],
            device_id=at(d, p),
            device_id_type=MESH,
        ).wait_recv()
        return c

    lax.fori_loop(1, 8, p_wait, 0)
    power = pow_r[0]
    for k in range(1, 8):
        power = power + pow_r[k]
    scale = to_col(lax.rsqrt(power[0:1, :] * (1.0 / WIDTH) + EPS))

    second(3)

    ld_cot.wait()

    def e_wait(i, c):
        p = (d + i) % NDP
        pltpu.make_async_remote_copy(
            src_ref=cr.at[p],
            dst_ref=cr.at[p],
            send_sem=esend.at[p],
            recv_sem=erecv.at[p],
            device_id=at(p, t),
            device_id_type=MESH,
        ).wait_recv()
        return c

    lax.fori_loop(1, NDP, e_wait, 0)

    finish_unit(2)
    slopes(0)
    finish_unit(1)
    spread(0)
    third(3)
    finish_unit(3)
    slopes(1)
    spread_far(0)
    spread(1)
    spread_end(0)
    reduce_core(0)
    spread_far(1)
    reduce_x(0)
    pvr[d] = pvs[d]
    lax.fori_loop(1, NDP, f_start, 0)
    spread_end(1)
    reduce_core(1)
    to_owner(0)
    reduce_x(1)
    to_owner(1)
    lax.fori_loop(1, NDP, f_wait, 0)
    pv_ref[0, 0] = pvr[...].reshape(NDP * SPAN, VW)
    finish(0)
    finish(1)

    for c in sent:
        c.wait_send()

    w_sent(0)
    w_sent(1)

    def p_done(i, c):
        p_copy((t + i) % 8).wait_send()
        return c

    def ef_done(i, c):
        e_copy((d + i) % NDP).wait_send()
        f_copy((d + i) % NDP).wait_send()
        return c

    lax.fori_loop(1, 8, p_done, 0)
    lax.fori_loop(1, NDP, ef_done, 0)
    for g in range(NG):
        for k in range(2):

            @pl.when(jnp.logical_not(fin_self(k)))
            def _():
                d_copy(g, k).wait_send()


def on_device(
    tokens,
    ref_gain,
    ref_weight,
    pol_gain,
    pol_weight,
    lengths,
    bins,
    advantage,
    logprob_gap,
    cotangent,
):
    any_spec = pl.BlockSpec(memory_space=pl.ANY)
    vmem = pl.BlockSpec(memory_space=pltpu.VMEM)
    smem = pl.BlockSpec(memory_space=pltpu.SMEM)
    dma = pltpu.SemaphoreType.DMA

    def buf(*shape, dtype=BF):
        return pltpu.VMEM(shape, dtype)

    return pl.pallas_call(
        kernel,
        out_shape=(
            jax.ShapeDtypeStruct(cotangent.shape, BF),
            jax.ShapeDtypeStruct((CHUNK, VW), F32),
        ),
        in_specs=[any_spec] * 4 + [vmem, vmem, smem, smem, smem, vmem],
        out_specs=(vmem, vmem),
        scratch_shapes=[
            buf(1024, FEAT),
            buf(FEAT, 1024),
            buf(FEAT, VW),
            buf(NG, FEAT, CW),
            buf(512, VW),
            buf(NG, FEAT, CW),
            buf(NG, FEAT, CW),
            buf(FEAT, 1, dtype=F32),
            buf(4, 2, 4, RB, CW),
            buf(4, 2, 2, HB, CW),
            buf(4, 2, 2, HB, CW),
            buf(4, 2, 2, HB, CW),
            buf(4, 3, 2, RB, CW),
            buf(4, 2, 2, HB, CW),
            buf(4, RB, CW),
            buf(4, RB, CW),
            buf(4, RB, CW, dtype=F32),
            buf(4, 4, RB, CW),
            buf(4, 4, RB, CW),
            buf(4, 2, HB, CW),
            buf(4, 2, HB, CW),
            buf(4, 2, HB, CW),
            buf(4, 2, HB, CW),
            buf(RB, VW, dtype=F32),
            buf(RB, VW, dtype=F32),
            buf(8, 8, RB, dtype=F32),
            buf(8, 8, RB, dtype=F32),
            buf(NDP, SPAN, VW),
            buf(NG, 2, 4, RB, CW),
            buf(NG, 2, 8, CHUNK, CW),
            buf(NG, 8, CHUNK, CW),
            buf(NG, 8, CHUNK, CW),
            buf(NG, 3, 2, CHUNK, CW),
            buf(NG, 2, CHUNK, CW),
            buf(NG, 2, CHUNK, CW),
            buf(NDP, SPAN, VW),
            buf(NDP, SPAN, VW),
            dma((4,)),
            dma((96,)),
            dma((96,)),
            dma((NG * 8,)),
            dma((NG * 8,)),
            dma((8,)),
            dma((8,)),
            dma((NDP,)),
            dma((NDP,)),
            dma((NDP,)),
            dma((NDP,)),
            dma((4,)),
            dma((4,)),
        ],
        compiler_params=pltpu.CompilerParams(collective_id=0, has_side_effects=True),
    )(
        tokens,
        ref_weight,
        pol_weight,
        cotangent,
        ref_gain.reshape(8, RB),
        pol_gain.reshape(8, 8, RB),
        lengths,
        bins,
        advantage,
        logprob_gap.reshape(1, RB),
    )


def solution(mesh):
    in_specs = (
        P("dp", "tensor"),
        P("tensor"),
        P("tensor", None),
        P(),
        P("dp", None),
        P("dp", "tensor", None),
        P("dp", "tensor", None),
        P("dp", "tensor", None),
        P(("dp", "tensor")),
        P("dp", "tensor", None, None),
    )
    out_specs = (P("dp", "tensor", None, None), P(("dp", "tensor"), None))
    return jax.shard_map(
        on_device, mesh=mesh, in_specs=in_specs, out_specs=out_specs, check_vma=False
    )
```

time: 86.7 us -> 76 us (0.88); the launches traced: 85.3 us -> 75.7 us
  Pallas kernels: 81.4 us -> 71.8 us
    pallas_call x1, Pallas kernels: 81.4 us -> 71.8 us  [on_device(): pl.pallas_call(kernel, out_shape=(jax.ShapeDtypeStruct(cotangent.shape, B...]
where the time goes in v2:
time: 76 us; the launch traced here: 75.7 us
  Pallas kernels  71.8 us (94%)
  local copies, waits for them, and re-layouts  3.24 us (4%)
    pallas_call x1, Pallas kernels, on_device(): pl.pallas_call(kernel, out_shape=(jax.ShapeDtypeStruct(cotangent.shape, B...  71.8 us
    unnamed x2, local copies, waits for them, and re-layouts  3.24 us

profile of v2, /device:TPU:24, one launch (start us, length us, event | category | flops | bytes accessed | tf_op | source)
XLA Modules:
  0.0 75.7 jit_solution(5515881878639817192)
XLA Ops:
  0.6 71.8 %shard_map.113 = (bf16[1,1,256,512]{3,2,1,0:T(8,128)(2,1)}, f32[64,512]{1,0:T(8,128)}) custom-call(bf16[1024,1024]{1,0:T(8,128)(2,1)} %x_hbm.1, bf16[1024,512]{1,0:T(8,128)(2,1)} %rw_hbm.1, bf16[512,512]{1,0:T(8,128)(2,1)} %pw_hbm.1, bf16[1,1,256,512]{3,2,1,0:T(8,128)(2,1)} %cot_hbm.1, f32[8,128]{1,0:T(8,128)} %bitcast.4, f32[8,8,128]{2,1,0:T(8,128)} %bitcast.3, ...), custom_call_target="tpu_custom_call" | custom-call | tf_op jit(solution)/shard_map/pallas_call | solution.py:769
  72.4 1.7 %copy.14 = bf16[1,1,256,512]{3,2,1,0:T(8,128)(2,1)} copy(bf16[1,1,256,512]{3,2,1,0:T(8,128)(2,1)} %get-tuple-element.4) | data formatting | bytes 524288
  74.1 1.6 %copy.15 = f32[64,512]{1,0:T(8,128)} copy(f32[64,512]{1,0:T(8,128)} %get-tuple-element.5) | data formatting | bytes 262144

commit v3 on v2

--- a/solution.py
+++ b/solution.py
@@ -23,7 +23,7 @@
 NDP = 16
 SPAN = 16
 AP = 64
-MODES = "yzee"
+MODES = "ezee"
 CHUNK = 64
 
 
@@ -614,6 +614,7 @@
         ).wait_recv()
         return c
 
+    lax.fori_loop(1, NDP, e_start, 0)
     second(0)
     def turn(i, c):
         cols = pl.ds(pl.multiple_of(i * CW, CW), CW)
@@ -651,7 +652,6 @@
     start(2)
     third(0)
     second(1)
-    lax.fori_loop(1, NDP, e_start, 0)
     w_share(1)
     policy(1)
     start(3)
@@ -746,6 +746,11 @@
                 d_copy(g, k).wait_send()
 
 
+def hand_over(packed_ref, grads_ref, pv_ref, gw_ref):
+    pv_ref[...] = packed_ref[...]
+    gw_ref[...] = grads_ref[...]
+
+
 def on_device(
     tokens,
     ref_gain,
@@ -766,7 +771,7 @@
     def buf(*shape, dtype=BF):
         return pltpu.VMEM(shape, dtype)
 
-    return pl.pallas_call(
+    packed, grads = pl.pallas_call(
         kernel,
         out_shape=(
             jax.ShapeDtypeStruct(cotangent.shape, BF),
@@ -839,6 +844,15 @@
         advantage,
         logprob_gap.reshape(1, RB),
     )
+    return pl.pallas_call(
+        hand_over,
+        out_shape=(
+            jax.ShapeDtypeStruct(cotangent.shape, BF),
+            jax.ShapeDtypeStruct((CHUNK, VW), F32),
+        ),
+        in_specs=[vmem, vmem],
+        out_specs=(vmem, vmem),
+    )(packed, grads)
 
 
 def solution(mesh):

time: 76 us -> 73.8 us (0.971)
  local copies, waits for them, and re-layouts: 3.24 us -> 0 us
  Pallas kernels: 71.8 us -> 73 us
    unnamed x2 -> x0, local copies, waits for them, and re-layouts: 3.24 us -> none
    pallas_call x0 -> x1, Pallas kernels: none -> 1.74 us  [on_device(): pl.pallas_call(hand_over, out_shape=(jax.ShapeDtypeStruct(cotangent.shape...]
where the time goes in v3:
time: 73.8 us; the launch traced here: 73.6 us
  Pallas kernels  73 us (99%)
    pallas_call x1, Pallas kernels, on_device(): pl.pallas_call(kernel, out_shape=(jax.ShapeDtypeStruct(cotangent.shape, B...  71.2 us
    pallas_call x1, Pallas kernels, on_device(): pl.pallas_call(hand_over, out_shape=(jax.ShapeDtypeStruct(cotangent.shape...  1.74 us

profile of v3, /device:TPU:24, one launch (start us, length us, event | category | flops | bytes accessed | tf_op | source)
XLA Modules:
  0.0 73.6 jit_solution(3224528381286936670)
XLA Ops:
  0.6 71.2 %shard_map.113 = (bf16[1,1,256,512]{3,2,1,0:T(8,128)(2,1)}, f32[64,512]{1,0:T(8,128)}) custom-call(bf16[1024,1024]{1,0:T(8,128)(2,1)} %x_hbm.1, bf16[1024,512]{1,0:T(8,128)(2,1)} %rw_hbm.1, bf16[512,512]{1,0:T(8,128)(2,1)} %pw_hbm.1, bf16[1,1,256,512]{3,2,1,0:T(8,128)(2,1)} %cot_hbm.1, f32[8,128]{1,0:T(8,128)} %bitcast.4, f32[8,8,128]{2,1,0:T(8,128)} %bitcast.3, ...), custom_call_target="tpu_custom_call" | custom-call | tf_op jit(solution)/shard_map/pallas_call | solution.py:774
  71.9 1.7 %shard_map.114 = (bf16[1,1,256,512]{3,2,1,0:T(8,128)(2,1)}, f32[64,512]{1,0:T(8,128)}) custom-call(bf16[1,1,256,512]{3,2,1,0:T(8,128)(2,1)} %get-tuple-element.4.packed_ref, f32[64,512]{1,0:T(8,128)} %get-tuple-element.5.grads_ref), custom_call_target="tpu_custom_call" | custom-call | tf_op jit(solution)/shard_map/pallas_call | solution.py:847

commit v4 on v3

--- a/solution.py
+++ b/solution.py
@@ -129,41 +129,42 @@
     ld_cot = pltpu.make_async_copy(
         cot_hbm.at[0, 0, pl.ds(pl.multiple_of(d * SPAN, SPAN), SPAN), :], cr.at[d], loc.at[3]
     )
+
+    bar = pltpu.get_barrier_semaphore()
+
+    def greet(dev):
+        pl.semaphore_signal(bar, inc=1, device_id=dev, device_id_type=MESH)
+
+    def greet_t(i, c):
+        greet(at(d, (t + i) % 8))
+        return c
+
+    def greet_d(i, c):
+        greet(at((d + i) % NDP, t))
+        return c
+
+
+    def greet_w(i, c):
+        @pl.when(jnp.logical_or(d // 2 != t, i != t))
+        def _():
+            greet(at(2 * t + core, i))
+
+        return c
+
+    lax.fori_loop(0, 8, greet_w, 0, unroll=True)
+
+    for s in range(2):
+
+        @pl.when(jnp.logical_not(jnp.logical_and(origin, zh == s)))
+        def _():
+            greet(fin_src(s))
+
+    lax.fori_loop(1, 8, greet_t, 0, unroll=True)
+    lax.fori_loop(1, NDP, greet_d, 0, unroll=True)
     ld_rw.start()
     ld_x.start()
     ld_pw.start()
     ld_cot.start()
-
-    bar = pltpu.get_barrier_semaphore()
-
-    def greet(dev):
-        pl.semaphore_signal(bar, inc=1, device_id=dev, device_id_type=MESH)
-
-    def greet_t(i, c):
-        greet(at(d, (t + i) % 8))
-        return c
-
-    def greet_d(i, c):
-        greet(at((d + i) % NDP, t))
-        return c
-
-    lax.fori_loop(1, 8, greet_t, 0)
-    lax.fori_loop(1, NDP, greet_d, 0)
-
-    def greet_w(i, c):
-        @pl.when(jnp.logical_or(d // 2 != t, i != t))
-        def _():
-            greet(at(2 * t + core, i))
-
-        return c
-
-    lax.fori_loop(0, 8, greet_w, 0)
-
-    for s in range(2):
-
-        @pl.when(jnp.logical_not(jnp.logical_and(origin, zh == s)))
-        def _():
-            greet(fin_src(s))
 
     eye = lax.broadcasted_iota(jnp.int32, (RB, RB), 0) == lax.broadcasted_iota(
         jnp.int32, (RB, RB), 1

time: 73.8 us -> 73.3 us (level)
  no operation moved by 1% of the time
where the time goes in v4:
time: 73.3 us; the launch traced here: 73.1 us
  Pallas kernels  72.4 us (99%)
    pallas_call x1, Pallas kernels, on_device(): pl.pallas_call(kernel, out_shape=(jax.ShapeDtypeStruct(cotangent.shape, B...  70.7 us
    pallas_call x1, Pallas kernels, on_device(): pl.pallas_call(hand_over, out_shape=(jax.ShapeDtypeStruct(cotangent.shape...  1.74 us

profile of v4, /device:TPU:24, one launch (start us, length us, event | category | flops | bytes accessed | tf_op | source)
XLA Modules:
  0.0 73.1 jit_solution(8001581006778815661)
XLA Ops:
  0.6 70.7 %shard_map.113 = (bf16[1,1,256,512]{3,2,1,0:T(8,128)(2,1)}, f32[64,512]{1,0:T(8,128)}) custom-call(bf16[1024,1024]{1,0:T(8,128)(2,1)} %x_hbm.1, bf16[1024,512]{1,0:T(8,128)(2,1)} %rw_hbm.1, bf16[512,512]{1,0:T(8,128)(2,1)} %pw_hbm.1, bf16[1,1,256,512]{3,2,1,0:T(8,128)(2,1)} %cot_hbm.1, f32[8,128]{1,0:T(8,128)} %bitcast.4, f32[8,8,128]{2,1,0:T(8,128)} %bitcast.3, ...), custom_call_target="tpu_custom_call" | custom-call | tf_op jit(solution)/shard_map/pallas_call | solution.py:775
  71.3 1.7 %shard_map.114 = (bf16[1,1,256,512]{3,2,1,0:T(8,128)(2,1)}, f32[64,512]{1,0:T(8,128)}) custom-call(bf16[1,1,256,512]{3,2,1,0:T(8,128)(2,1)} %get-tuple-element.4.packed_ref, f32[64,512]{1,0:T(8,128)} %get-tuple-element.5.grads_ref), custom_call_target="tpu_custom_call" | custom-call | tf_op jit(solution)/shard_map/pallas_call | solution.py:848

commit v5 on v4

--- a/solution.py
+++ b/solution.py
@@ -454,7 +454,7 @@
         p_copy((t + i) % 8).start()
         return c
 
-    lax.fori_loop(1, 8, p_start, 0)
+    lax.fori_loop(1, 8, p_start, 0, unroll=True)
 
 
     def e_copy(peer):
@@ -488,8 +488,8 @@
         slope = coef_adv * upstream + coef_pull * (values - ref_values)
         ss[g, zl, y0] = (slope * scale).astype(BF)
         mine = ss.at[g, zl, y0]
+        copy(("cz", g), mine, mine, zp)
         copy(("cf", g), mine, mine, yf)
-        copy(("cz", g), mine, mine, zp)
         copy(("cp", g), mine, mine, yp)
         copy(("cm", g), mine, mine, ym)
         out = jnp.dot(place, values.astype(BF), preferred_element_type=F32).astype(BF)
@@ -615,7 +615,7 @@
         ).wait_recv()
         return c
 
-    lax.fori_loop(1, NDP, e_start, 0)
+    lax.fori_loop(1, NDP, e_start, 0, unroll=True)
     second(0)
     def turn(i, c):
         cols = pl.ds(pl.multiple_of(i * CW, CW), CW)
@@ -711,7 +711,7 @@
     spread_far(1)
     reduce_x(0)
     pvr[d] = pvs[d]
-    lax.fori_loop(1, NDP, f_start, 0)
+    lax.fori_loop(1, NDP, f_start, 0, unroll=True)
     spread_end(1)
     reduce_core(1)
     to_owner(0)

time: 73.3 us -> 73.3 us (level)
  no operation moved by 1% of the time
where the time goes in v5:
time: 73.3 us; the launch traced here: 73.1 us
  Pallas kernels  72.5 us (99%)
    pallas_call x1, Pallas kernels, on_device(): pl.pallas_call(kernel, out_shape=(jax.ShapeDtypeStruct(cotangent.shape, B...  70.7 us
    pallas_call x1, Pallas kernels, on_device(): pl.pallas_call(hand_over, out_shape=(jax.ShapeDtypeStruct(cotangent.shape...  1.74 us

profile of v5, /device:TPU:24, one launch (start us, length us, event | category | flops | bytes accessed | tf_op | source)
XLA Modules:
  0.0 73.1 jit_solution(9898550052128332791)
XLA Ops:
  0.6 70.7 %shard_map.113 = (bf16[1,1,256,512]{3,2,1,0:T(8,128)(2,1)}, f32[64,512]{1,0:T(8,128)}) custom-call(bf16[1024,1024]{1,0:T(8,128)(2,1)} %x_hbm.1, bf16[1024,512]{1,0:T(8,128)(2,1)} %rw_hbm.1, bf16[512,512]{1,0:T(8,128)(2,1)} %pw_hbm.1, bf16[1,1,256,512]{3,2,1,0:T(8,128)(2,1)} %cot_hbm.1, f32[8,128]{1,0:T(8,128)} %bitcast.4, f32[8,8,128]{2,1,0:T(8,128)} %bitcast.3, ...), custom_call_target="tpu_custom_call" | custom-call | tf_op jit(solution)/shard_map/pallas_call | solution.py:775
  71.4 1.7 %shard_map.114 = (bf16[1,1,256,512]{3,2,1,0:T(8,128)(2,1)}, f32[64,512]{1,0:T(8,128)}) custom-call(bf16[1,1,256,512]{3,2,1,0:T(8,128)(2,1)} %get-tuple-element.4.packed_ref, f32[64,512]{1,0:T(8,128)} %get-tuple-element.5.grads_ref), custom_call_target="tpu_custom_call" | custom-call | tf_op jit(solution)/shard_map/pallas_call | solution.py:848

commit v6 on v5

--- a/solution.py
+++ b/solution.py
@@ -371,7 +371,7 @@
 
             return c
 
-        lax.fori_loop(0, 8, step, 0)
+        lax.fori_loop(0, 8, step, 0, unroll=True)
 
     def w_sent(g):
         def step(i, c):

time: 73.3 us -> 73.3 us (level)
  no operation moved by 1% of the time
where the time goes in v6:
time: 73.3 us; the launch traced here: 73.1 us
  Pallas kernels  72.5 us (99%)
    pallas_call x1, Pallas kernels, on_device(): pl.pallas_call(kernel, out_shape=(jax.ShapeDtypeStruct(cotangent.shape, B...  70.7 us
    pallas_call x1, Pallas kernels, on_device(): pl.pallas_call(hand_over, out_shape=(jax.ShapeDtypeStruct(cotangent.shape...  1.74 us

profile of v6, /device:TPU:24, one launch (start us, length us, event | category | flops | bytes accessed | tf_op | source)
XLA Modules:
  0.0 73.1 jit_solution(13525246798925082065)
XLA Ops:
  0.6 70.7 %shard_map.113 = (bf16[1,1,256,512]{3,2,1,0:T(8,128)(2,1)}, f32[64,512]{1,0:T(8,128)}) custom-call(bf16[1024,1024]{1,0:T(8,128)(2,1)} %x_hbm.1, bf16[1024,512]{1,0:T(8,128)(2,1)} %rw_hbm.1, bf16[512,512]{1,0:T(8,128)(2,1)} %pw_hbm.1, bf16[1,1,256,512]{3,2,1,0:T(8,128)(2,1)} %cot_hbm.1, f32[8,128]{1,0:T(8,128)} %bitcast.4, f32[8,8,128]{2,1,0:T(8,128)} %bitcast.3, ...), custom_call_target="tpu_custom_call" | custom-call | tf_op jit(solution)/shard_map/pallas_call | solution.py:775
  71.4 1.7 %shard_map.114 = (bf16[1,1,256,512]{3,2,1,0:T(8,128)(2,1)}, f32[64,512]{1,0:T(8,128)}) custom-call(bf16[1,1,256,512]{3,2,1,0:T(8,128)(2,1)} %get-tuple-element.4.packed_ref, f32[64,512]{1,0:T(8,128)} %get-tuple-element.5.grads_ref), custom_call_target="tpu_custom_call" | custom-call | tf_op jit(solution)/shard_map/pallas_call | solution.py:848
